TPU v7x, 32 devices: a whole 2x2x4 slice. The times are simulated.
32 devices in a mesh: seq: 8 (over y, x, core), dp: 4 (over z).
Axes of the slice: x: 2, y: 2, z: 4, core: 2. Of those that a mesh axis runs over, the one named last changes fastest.
Arguments:
- tokens: bfloat16 [4, 2048, 2048], P('dp', 'seq'), may hold values from -6 to 6
- w_qkv: bfloat16 [2048, 3, 1024], P('seq'), may hold values from -0.125 to 0.125
- weight_table: float32 [16, 8], replicated, may hold values from 0.3 to 3
- weight_index: int32 [4, 16, 4], P('dp', 'seq'), may hold values from 0 to 15
- cotangent: bfloat16 [4, 2048, 1024], P('dp', 'seq'), may hold values from -6 to 6
Outputs:
- attn_out: bfloat16 [4, 2048, 1024], P('dp', 'seq')
- grad_w: float32 [2048, 3, 1024], P('seq')
All inputs are finite; a program needn't handle non-finite values.
Results may differ from a plain program's by a relative error of at most 0.02.
Values may be sent and summed in bfloat16 or wider, within the bound.
A program may use at most 128 MiB of HBM per device.

v0:
```python
import functools
import math

import jax
import jax.numpy as jnp
from jax import lax
from jax.experimental import pallas as pl
from jax.experimental.pallas import tpu as pltpu
from jax.sharding import PartitionSpec as P


def swapped(value, axis, bit):
    mask = 2**bit
    pairs = [(source, source ^ mask) for source in range(lax.axis_size(axis))]
    return lax.ppermute(value, axis, pairs)


def level_factors(weight_table, weight_index, block_len):
    table_rows = weight_table.shape[0]
    chosen = weight_index[0]
    onehot = (chosen[:, :, None] == jnp.arange(table_rows, dtype=jnp.int32)[None, None, :]).astype(
        jnp.float32
    )
    per_block = jnp.einsum("blw,wh->blh", onehot, weight_table, precision=lax.Precision.HIGHEST)
    groups = chosen.shape[0]
    spread = jnp.broadcast_to(
        per_block[:, None], (groups, block_len // groups, chosen.shape[1], weight_table.shape[1])
    )
    return spread.reshape(block_len, chosen.shape[1], weight_table.shape[1])


def make_adder(inputs, columns, shard_rows):
    flat_rows = shard_rows.reshape(shard_rows.shape[0], columns)
    return jnp.dot(inputs, flat_rows, preferred_element_type=jnp.float32)


def climb(keys_bf, values_bf, levels):
    running = jnp.einsum("shd,she->hde", keys_bf, values_bf, preferred_element_type=jnp.float32)
    partners = []
    for bit_pos in range(levels):
        partner = swapped(running.astype(jnp.bfloat16), "seq", bit_pos).astype(running.dtype)
        partners.append(partner)
        running = running + partner
    return partners


def descend(level_grads, levels, device):
    carried = [level_grads[:, bit_pos] for bit_pos in range(levels)]
    gathered = jnp.zeros_like(level_grads[:, 0])
    for bit_pos in range(levels):
        outgoing = jnp.stack(carried[bit_pos:], axis=1)
        incoming = swapped(outgoing.astype(jnp.bfloat16), "seq", bit_pos).astype(outgoing.dtype)
        keeping = (1 - device // 2**bit_pos % 2).astype(jnp.float32)
        gathered = gathered + keeping * incoming[:, 0]
        for upper in range(bit_pos + 1, levels):
            carried[upper] = carried[upper] + incoming[:, upper - bit_pos]
    return gathered


def per_device(tokens, w_qkv, weight_table, weight_index, cotangent):
    inputs = tokens[0]
    block_len = inputs.shape[0]
    inner_width = w_qkv.shape[2]
    head_count = weight_table.shape[1]
    head_dim = inner_width // head_count
    levels = lax.axis_size("seq").bit_length() - 1
    device = lax.axis_index("seq")
    projected = make_adder(
        inputs, 3 * inner_width, lax.all_gather(w_qkv, "seq", axis=0, tiled=True)
    )
    projected = projected.astype(jnp.bfloat16).reshape(block_len, 3, head_count, head_dim)
    queries = projected[:, 0]
    keys_bf = projected[:, 1]
    values_bf = projected[:, 2]
    partners = climb(keys_bf, values_bf, levels)
    level_states = jnp.stack(partners, axis=2).astype(jnp.bfloat16)
    powers = 2 ** jnp.arange(levels, dtype=jnp.int32)
    bit_flags = (device // powers % 2).astype(jnp.float32)
    halves = 2.0 ** jnp.arange(levels, dtype=jnp.float32)
    scale_level = bit_flags / jnp.sqrt(head_dim * halves * block_len)
    weights_tok = level_factors(weight_table, weight_index, block_len)
    level_coef = jnp.transpose(weights_tok[:, 1 : levels + 1, :], (0, 2, 1)) * scale_level
    local_scale = weights_tok[:, 0, :] / math.sqrt(head_dim * block_len)
    row_scale = jnp.transpose(local_scale)[:, :, None]
    causal = jnp.arange(block_len)[:, None] >= jnp.arange(block_len)[None, :]
    raw_scores = jnp.einsum("thd,shd->hts", queries, keys_bf, preferred_element_type=jnp.float32)
    scores = jnp.where(causal[None], raw_scores * row_scale, 0.0).astype(jnp.bfloat16)
    local_out = jnp.einsum("hts,she->the", scores, values_bf, preferred_element_type=jnp.float32)
    far_terms = jnp.einsum(
        "thd,hdle->thle", queries, level_states, preferred_element_type=jnp.float32
    )
    attended = local_out + jnp.sum(far_terms * level_coef[..., None], axis=2)
    attn_out = attended.astype(jnp.bfloat16).reshape(1, block_len, inner_width)
    upstream = cotangent[0].reshape(block_len, head_count, head_dim)
    raw_grads = jnp.einsum("the,she->hts", upstream, values_bf, preferred_element_type=jnp.float32)
    dscores = jnp.where(causal[None], raw_grads * row_scale, 0.0).astype(jnp.bfloat16)
    far_grads = jnp.einsum(
        "the,hdle->thld", upstream, level_states, preferred_element_type=jnp.float32
    )
    grad_q = jnp.einsum("hts,shd->thd", dscores, keys_bf, preferred_element_type=jnp.float32)
    grad_q = grad_q + jnp.sum(far_grads * level_coef[..., None], axis=2)
    grad_k = jnp.einsum("hts,thd->shd", dscores, queries, preferred_element_type=jnp.float32)
    grad_v = jnp.einsum("hts,the->she", scores, upstream, preferred_element_type=jnp.float32)
    scaled = (queries.astype(jnp.float32)[:, :, None, :] * level_coef[..., None]).astype(
        jnp.bfloat16
    )
    level_grads = jnp.einsum("thld,the->hlde", scaled, upstream, preferred_element_type=jnp.float32)
    state_grads = descend(level_grads, levels, device).astype(jnp.bfloat16)
    grad_k = grad_k + jnp.einsum(
        "she,hde->shd", values_bf, state_grads, preferred_element_type=jnp.float32
    )
    grad_v = grad_v + jnp.einsum(
        "shd,hde->she", keys_bf, state_grads, preferred_element_type=jnp.float32
    )
    qkv_grads = (
        jnp.stack([grad_q, grad_k, grad_v], axis=1)
        .astype(jnp.bfloat16)
        .reshape(block_len, 3 * inner_width)
    )
    shard_rows = w_qkv.shape[0]
    partial_value = jnp.einsum("tr,tc->rc", inputs, qkv_grads, preferred_element_type=jnp.float32)
    seq_sum = lax.psum_scatter(
        partial_value.reshape(lax.axis_size("seq") * shard_rows, 3, inner_width).astype(
            jnp.bfloat16
        ),
        "seq",
        scatter_dimension=0,
        tiled=True,
    )
    grad_w = lax.psum(seq_sum, "dp").astype(jnp.float32)
    return (attn_out, grad_w)

def head_parallel(tokens, w_qkv, weight_table, weight_index, cotangent):
    seq = lax.axis_size("seq")
    me = lax.axis_index("seq")
    inputs = tokens[0]
    block_len = inputs.shape[0]
    inner_width = w_qkv.shape[2]
    head_count = weight_table.shape[1]
    head_dim = inner_width // head_count
    own = head_count // seq
    levels = seq.bit_length() - 1
    rows = w_qkv.shape[0]
    bf = jnp.bfloat16
    f32 = jnp.float32
    every = lax.all_gather(inputs, "seq", axis=0, tiled=True)
    w_cols = w_qkv.reshape(rows, 3, seq, own * head_dim)
    w_cols = lax.all_to_all(w_cols, "seq", split_axis=2, concat_axis=0)
    w_cols = w_cols.reshape(seq * rows, 3 * own * head_dim)
    up = cotangent[0].reshape(block_len, seq, own * head_dim)
    up = lax.all_to_all(up, "seq", split_axis=1, concat_axis=0)
    up = up.reshape(seq, block_len, own, head_dim)
    chosen = lax.all_gather(weight_index[0], "seq", axis=0, tiled=True)
    table = lax.dynamic_slice_in_dim(weight_table, me * own, own, axis=1)
    lam = table[chosen]
    groups = chosen.shape[0]
    lam = jnp.repeat(lam, seq * block_len // groups, axis=0)
    lam = lam.reshape(seq, block_len, levels + 1, own)
    qkv = jnp.dot(every, w_cols, preferred_element_type=f32).astype(bf)
    qkv = qkv.reshape(seq, block_len, 3, own, head_dim)
    q, k, v = qkv[:, :, 0], qkv[:, :, 1], qkv[:, :, 2]

    def prod(pattern, a, b):
        return jnp.einsum(pattern, a, b, preferred_element_type=f32)

    states = prod("pshd,pshe->phde", k, v)
    scale0 = jnp.transpose(lam[:, :, 0], (0, 2, 1))[..., None] / math.sqrt(head_dim * block_len)
    causal = jnp.arange(block_len)[:, None] >= jnp.arange(block_len)[None, :]
    scores = jnp.where(causal, prod("pthd,pshd->phts", q, k) * scale0, 0.0).astype(bf)
    dscores = jnp.where(causal, prod("pthd,pshd->phts", up, v) * scale0, 0.0).astype(bf)
    out = prod("phts,pshe->pthe", scores, v)
    grad_q = prod("phts,pshd->pthd", dscores, k)
    grad_k = prod("phts,pthd->pshd", dscores, q)
    grad_v = prod("phts,pthe->pshe", scores, up)
    state_grads = jnp.zeros((seq, own, head_dim, head_dim), f32)
    for level in range(1, levels + 1):
        half = 2 ** (level - 1)
        shape = (seq // (2 * half), 2, half)
        tail = (own, head_dim, head_dim)
        level_state = jnp.sum(states.reshape(shape + tail)[:, 0], axis=1).astype(bf)
        coef = (lam[:, :, level] / math.sqrt(head_dim * half * block_len))[..., None]

        def right(value):
            return value.reshape(shape + value.shape[1:])[:, 1]

        q_r, up_r, coef_r = right(q), right(up), right(coef)
        far = prod("gjthd,ghde->gjthe", q_r, level_state) * coef_r
        far_q = prod("gjthe,ghde->gjthd", up_r, level_state) * coef_r
        scaled = (q_r.astype(f32) * coef_r).astype(bf)
        grads = prod("gjthd,gjthe->ghde", scaled, up_r)

        def spread(value, side):
            zero = jnp.zeros_like(value)
            pair = [value, zero] if side == 0 else [zero, value]
            return jnp.stack(pair, axis=1).reshape((seq,) + value.shape[2:])

        out = out + spread(far, 1)
        grad_q = grad_q + spread(far_q, 1)
        wide = jnp.broadcast_to(grads[:, None], (grads.shape[0], half) + tail)
        state_grads = state_grads + spread(wide, 0)
    state_grads = state_grads.astype(bf)
    grad_k = grad_k + prod("pshe,phde->pshd", v, state_grads)
    grad_v = grad_v + prod("pshd,phde->pshe", k, state_grads)
    grads = jnp.stack([grad_q, grad_k, grad_v], axis=2).astype(bf)
    grads = grads.reshape(seq * block_len, 3 * own * head_dim)
    out = out.astype(bf).reshape(seq, block_len, own * head_dim)
    out = lax.all_to_all(out, "seq", split_axis=0, concat_axis=1)
    attn_out = out.reshape(1, block_len, inner_width)
    grad_w = prod("tr,tc->rc", every, grads).astype(bf)
    grad_w = grad_w.reshape(seq, rows, 3, own * head_dim)
    grad_w = lax.all_to_all(grad_w, "seq", split_axis=0, concat_axis=2)
    grad_w = grad_w.reshape(rows, 3, inner_width)
    grad_w = lax.psum(grad_w, "dp").astype(f32)
    return (attn_out, grad_w)

def flip(index, mask):
    result = index
    for bit in (1, 2, 4):
        chosen = lax.rem(lax.div(mask, bit), 2) if not isinstance(mask, int) else mask // bit % 2
        result = result + chosen * (bit - 2 * bit * lax.rem(lax.div(index, bit), 2))
    return result


def dims(a, b, da, db):
    return lax.dot_general(a, b, (((da,), (db,)), ((), ())), preferred_element_type=jnp.float32)


def fused_kernel(
    sizes,
    tok_ref, w_ref, table_ref, index_ref, cot_ref,
    out_ref, gw_ref,
    lam_ref, xs, xt, wh, cs, lam, qkv, st, loc, outf, outb, dqkv, lvl, gl,
    gs, own, leaf, pair, pairb, fin,
    s_local, s_ws, s_wr, s_cs, s_cr, s_ls, s_lr, s_xs, s_xr, s_os, s_or,
    s_wa, s_war, s_wb, s_wbr, s_wc, s_wcr, s_gs, s_gr, s_za, s_zar, s_zb, s_zbr, s_zc, s_zcr, s_fin,
):
    seq, dp, block, width, hd, groups, levels, parts, subs, lag = sizes
    bf = jnp.bfloat16
    f32 = jnp.float32
    me = lax.axis_index("seq")
    z = lax.axis_index("dp")
    core = lax.rem(me, 2)
    first = 2 + 2 * core
    other = 4 - 2 * core
    rows = width // seq
    part = block // parts
    piece_rows = rows // subs

    def remote(src, dst, ssem, rsem, peer):
        return pltpu.make_async_remote_copy(
            src_ref=src, dst_ref=dst, send_sem=ssem, recv_sem=rsem,
            device_id=peer, device_id_type=pl.DeviceIdType.MESH,
        )

    def lanes(index):
        return pl.ds(pl.multiple_of(index * hd, hd), hd)

    def span(index, size):
        return pl.ds(pl.multiple_of(index * size, size), size)

    barrier = pltpu.get_barrier_semaphore()
    for mask in range(1, seq):
        pl.semaphore_signal(
            barrier, inc=1, device_id={"seq": flip(me, mask)}, device_id_type=pl.DeviceIdType.MESH
        )
    for step in range(1, dp):
        pl.semaphore_signal(
            barrier, inc=1, device_id={"dp": lax.rem(z + step, dp)},
            device_id_type=pl.DeviceIdType.MESH,
        )
    for level in range(levels + 1):
        factor = jnp.float32(1 / math.sqrt(hd * block))
        if level > 0:
            bit = 2 ** (level - 1)
            flag = lax.rem(lax.div(me, bit), 2).astype(f32)
            factor = flag * jnp.float32(1 / math.sqrt(hd * bit * block))
        for g in range(groups):
            row = index_ref[g, level]
            for h in range(seq):
                lam_ref[h, pl.ds(level * groups + g, 1), :] = jnp.full(
                    (1, hd), table_ref[h, row] * factor, f32
                )
    pl.semaphore_wait(barrier, seq - 1 + dp - 1)

    inner = lax.rem(lax.div(z + 1, 2), 2) == 1
    mate = jnp.where(z < dp // 2, 1 - z, 5 - z)
    cross = 3 - z
    side = lax.div(z, 2)
    quarter = rows // dp
    half_rows = rows // 2

    def held(source, start, count):
        return pl.ds(pl.multiple_of(source * rows + start, quarter), count)

    def w_copy(mask, i):
        peer = flip(me, mask)
        near = mask == 1
        start, count = (0, rows) if near else (z * quarter, quarter)
        return remote(
            w_ref.at[i, pl.ds(pl.multiple_of(start, quarter), count), lanes(peer)],
            wh.at[held(me, start, count), pl.ds(i * hd, hd)],
            s_ws.at[mask, i], s_wr.at[mask, i], {"seq": peer},
        )

    def wa_copy(mask):
        piece = wh.at[held(flip(me, mask), z * quarter, quarter)]
        return remote(piece, piece, s_wa.at[mask], s_war.at[mask], {"dp": mate})

    def wb_copy(mask):
        piece = wh.at[held(flip(me, mask), side * half_rows, half_rows)]
        return remote(piece, piece, s_wb.at[mask], s_wbr.at[mask], {"dp": cross})

    def wc_copy(mask):
        piece = wh.at[held(flip(me, mask), (1 - side) * half_rows, half_rows)]
        return remote(piece, piece, s_wc.at[mask], s_wcr.at[mask], {"dp": mate})

    def l_copy(mask):
        peer = flip(me, mask)
        return remote(lam_ref.at[peer], lam.at[me], s_ls.at[mask], s_lr.at[mask], {"seq": peer})

    def c_copy(mask):
        peer = flip(me, mask)
        return remote(
            cot_ref.at[:, lanes(peer)], cs.at[me], s_cs.at[mask], s_cr.at[mask], {"seq": peer}
        )

    def x_first(mask, j):
        piece = pl.ds(j * part, part)
        return remote(
            tok_ref.at[piece], xs.at[me, piece],
            s_xs.at[mask, j], s_xr.at[mask, j], {"seq": flip(me, mask)},
        )

    def x_relay(j):
        piece = pl.ds(j * part, part)
        moved = flip(me, first)
        return remote(
            xs.at[moved, piece], xs.at[moved, piece],
            s_xs.at[6, j], s_xr.at[6, j], {"seq": flip(me, other)},
        )

    def x_across(mask, j):
        piece = pl.ds(j * part, part)
        moved = flip(me, mask)
        return remote(
            xs.at[moved, piece], xs.at[moved, piece],
            s_xs.at[mask + 1, j], s_xr.at[mask + 1, j], {"seq": flip(me, 1)},
        )

    def x_arrived(mask, j):
        piece = pl.ds(j * part, part)
        moved = flip(me, mask)
        return remote(
            xs.at[moved, piece], xs.at[moved, piece],
            s_xs.at[0, j], s_xr.at[mask, j], {"seq": flip(me, 1)},
        )

    locals_ = [
        pltpu.make_async_copy(tok_ref, xs.at[me], s_local.at[0]),
        pltpu.make_async_copy(cot_ref.at[:, lanes(me)], cs.at[me], s_local.at[1]),
        pltpu.make_async_copy(lam_ref.at[me], lam.at[me], s_local.at[2]),
    ]
    for i in range(3):
        locals_.append(
            pltpu.make_async_copy(
                w_ref.at[i, :, lanes(me)], wh.at[span(me, rows), pl.ds(i * hd, hd)],
                s_local.at[3 + i],
            )
        )
    order = (6, 7, 2, 3, 4, 5, 1)
    for mask in order:
        l_copy(mask).start()
        for i in range(3):
            w_copy(mask, i).start()
    for mask in order:
        c_copy(mask).start()
    for j in range(parts):
        for mask in (2, 4, 1):
            x_first(mask, j).start()
    for copy in locals_:
        copy.start()
    for copy in locals_:
        copy.wait()
    far_masks = order[:-1]
    for mask in far_masks:
        for i in range(3):
            w_copy(mask, i).wait_recv()
        wa_copy(mask).start()

    @pl.when(inner)
    def _():
        for mask in far_masks:
            wa_copy(mask).wait_recv()
            wb_copy(mask).start()
        for mask in far_masks:
            wb_copy(mask).wait_recv()
            wc_copy(mask).start()

    @pl.when(jnp.logical_not(inner))
    def _():
        for mask in far_masks:
            wa_copy(mask).wait_recv()
        for mask in far_masks:
            wc_copy(mask).wait_recv()

    for i in range(3):
        w_copy(1, i).wait_recv()
    for mask in order:
        l_copy(mask).wait_recv()
        c_copy(mask).wait_recv()

    tri = lax.broadcasted_iota(jnp.int32, (block, block), 0) >= lax.broadcasted_iota(
        jnp.int32, (block, block), 1
    )

    def coef(p, level):
        pieces = []
        for g in range(groups):
            row = lam[p, pl.ds(level * groups + g, 1), :]
            pieces.append(jnp.broadcast_to(row, (block // groups, hd)))
        return jnp.concatenate(pieces, axis=0)

    def local_block(i, carry):
        half = lax.div(i, 2)
        low = lax.rem(i, 2)
        mask = jnp.where(
            half == 0, low,
            jnp.where(
                half == 1, first + low * (other - first),
                jnp.where(half == 2, 1 + other + low * (first - other), 6 + low),
            ),
        )
        p = flip(me, mask)

        @pl.when(i == 1)
        def _():
            for j in range(parts):
                x_arrived(1, j).wait_recv()

        @pl.when(i == 2)
        def _():
            for j in range(parts):
                x_arrived(first, j).wait_recv()
                x_relay(j).start()
                x_across(first, j).start()
                x_arrived(other, j).wait_recv()
                x_across(other, j).start()

        @pl.when(half == 2)
        def _():
            for j in range(parts):
                x_arrived(mask, j).wait_recv()

        @pl.when(i == 6)
        def _():
            for j in range(parts):
                x_arrived(6, j).wait_recv()
                x_across(6, j).start()

        @pl.when(i == 7)
        def _():
            for j in range(parts):
                x_arrived(7, j).wait_recv()

        x = xs[p]
        proj = dims(x, wh[...], 1, 0).astype(bf)
        qkv[p] = proj
        xt[:, span(p, block)] = x.T
        q, k, v = proj[:, :hd], proj[:, hd : 2 * hd], proj[:, 2 * hd :]
        c = cs[p]
        st[p] = dims(k, v, 0, 0)
        scale = coef(p, 0)
        scale = jnp.concatenate([scale] * (block // hd), axis=1)
        scores = jnp.where(tri, dims(q, k, 1, 1) * scale, 0.0).astype(bf)
        dscores = jnp.where(tri, dims(c, v, 1, 1) * scale, 0.0).astype(bf)
        outf[p] = dims(scores, v, 1, 0)
        loc[p, :, pl.ds(0, hd)] = dims(dscores, k, 1, 0)
        loc[p, :, pl.ds(hd, hd)] = dims(dscores, q, 0, 0)
        loc[p, :, pl.ds(2 * hd, hd)] = dims(scores, c, 0, 0)
        return carry

    lax.fori_loop(0, seq, local_block, 0)

    level_sum = {}
    for level in range(1, levels + 1):
        half = 2 ** (level - 1)
        for base in range(0, seq, 2 * half):
            total = st[base]
            for j in range(1, half):
                total = total + st[base + j]
            lvl[level - 1, base] = total.astype(bf)

    def o_copy(mask):
        peer = flip(me, mask)
        return remote(
            outb.at[peer], out_ref.at[:, lanes(me)], s_os.at[mask], s_or.at[mask], {"seq": peer}
        )

    blank = jnp.zeros((hd, hd), bf)

    def joined(a, b, c, d):
        top = jnp.concatenate([a, b], axis=1)
        return jnp.concatenate([top, jnp.concatenate([c, d], axis=1)], axis=0)

    for level in range(1, levels + 1):
        half = 2 ** (level - 1)
        for base in range(0, seq, 2 * half):
            state = lvl[level - 1, base]
            both = joined(state, blank, blank, state.T)
            total = None
            for p in range(base + half, base + 2 * half):
                q = qkv[p, :, pl.ds(0, hd)]
                c = cs[p]
                factor = coef(p, level)
                far = dims(jnp.concatenate([q, c], axis=1), both, 1, 0)
                outf[p] += far[:, :hd] * factor
                loc[p, :, pl.ds(0, hd)] += far[:, hd:] * factor
                scaled = (q.astype(f32) * factor).astype(bf)
                grads = dims(scaled, c, 0, 0)
                total = grads if total is None else total + grads
            gl[level - 1, base] = total
    for p in range(seq):
        outb[p] = outf[p].astype(bf)
    for mask in range(1, seq):
        o_copy(mask).start()
    o_local = pltpu.make_async_copy(outb.at[me], out_ref.at[:, lanes(me)], s_local.at[6])
    o_local.start()
    for p in range(seq):
        total = None
        for level in range(1, levels + 1):
            half = 2 ** (level - 1)
            if p // half % 2 == 0:
                base = p - p % (2 * half)
                term = gl[level - 1, base]
                total = term if total is None else total + term
        grads = loc[p, :, pl.ds(hd, 2 * hd)]
        if total is not None:
            g = total.astype(bf)
            both = joined(blank, g, g.T, blank)
            grads = grads + dims(qkv[p, :, pl.ds(hd, 2 * hd)], both, 1, 0)
        spot = pl.ds(p * block, block)
        dqkv[spot, pl.ds(0, hd)] = loc[p, :, pl.ds(0, hd)].astype(bf)
        dqkv[spot, pl.ds(hd, 2 * hd)] = grads.astype(bf)

    def g_copy(m):
        return remote(gs.at[m], own.at[m], s_gs.at[m], s_gr.at[m], {"seq": flip(me, m)})

    def bit_of(r):
        return pl.ds(pl.multiple_of(lax.rem(r, subs) * piece_rows, piece_rows), piece_rows)

    def za_copy(r):
        m, at = lax.div(r, subs), bit_of(r)
        return remote(own.at[m, at], leaf.at[m, at], s_za.at[r], s_zar.at[r], {"dp": mate})

    def zb_copy(r):
        m, at = lax.div(r, subs), bit_of(r)
        return remote(pair.at[m, at], pairb.at[m, at], s_zb.at[r], s_zbr.at[r], {"dp": cross})

    def zc_copy(r):
        m, at = lax.div(r, subs), bit_of(r)
        return remote(fin.at[m, at], fin.at[m, at], s_zc.at[r], s_zcr.at[r], {"dp": mate})

    def fin_copy(m, i):
        return pltpu.make_async_copy(
            fin.at[m, :, pl.ds(i * hd, hd)], gw_ref.at[i, :, lanes(flip(me, m))], s_fin.at[m, i]
        )

    steps = seq * subs

    def reduce_round(t, carry):
        m = lax.div(t, subs)

        @pl.when((t < steps) & (lax.rem(t, subs) == 0))
        def _():
            o = flip(me, m)
            chunk = dims(xt[span(o, rows), :], dqkv[...], 1, 0).astype(bf)

            @pl.when(m == 0)
            def _():
                own[0] = chunk

            @pl.when(m > 0)
            def _():
                gs[m] = chunk
                g_copy(m).start()

        @pl.when((t >= subs) & (t < steps + subs))
        def _():
            r = t - subs
            done = lax.div(r, subs)
            at = bit_of(r)

            @pl.when((r >= subs) & (lax.rem(r, subs) == 0))
            def _():
                g_copy(done).wait_recv()

            @pl.when(jnp.logical_not(inner))
            def _():
                za_copy(r).start()

            @pl.when(inner)
            def _():
                za_copy(r).wait_recv()
                pair[done, at] = (own[done, at].astype(f32) + leaf[done, at].astype(f32)).astype(bf)
                zb_copy(r).start()

        @pl.when((t >= subs + lag) & inner)
        def _():
            r = t - subs - lag
            done = lax.div(r, subs)
            at = bit_of(r)
            zb_copy(r).wait_recv()
            fin[done, at] = (pair[done, at].astype(f32) + pairb[done, at].astype(f32)).astype(bf)
            zc_copy(r).start()

            @pl.when(lax.rem(r, subs) == subs - 1)
            def _():
                for i in range(3):
                    fin_copy(done, i).start()

        return carry

    lax.fori_loop(0, steps + subs + lag, reduce_round, 0)

    @pl.when(jnp.logical_not(inner))
    def _():
        def collect(m, carry):
            for b in range(subs):
                zc_copy(m * subs + b).wait_recv()
            for i in range(3):
                fin_copy(m, i).start()
            for b in range(subs):
                za_copy(m * subs + b).wait_send()
            return carry

        lax.fori_loop(0, seq, collect, 0)

    @pl.when(inner)
    def _():
        def settle(r, carry):
            zb_copy(r).wait_send()
            zc_copy(r).wait_send()
            return carry

        lax.fori_loop(0, steps, settle, 0)

    for mask in far_masks:
        wa_copy(mask).wait_send()

    @pl.when(inner)
    def _():
        for mask in far_masks:
            wb_copy(mask).wait_send()
            wc_copy(mask).wait_send()

    for m in range(seq):
        for i in range(3):
            fin_copy(m, i).wait()
    o_local.wait()
    for mask in range(1, seq):
        o_copy(mask).wait_send()
        o_copy(mask).wait_recv()
        g_copy(mask).wait_send()
        l_copy(mask).wait_send()
        c_copy(mask).wait_send()
        for i in range(3):
            w_copy(mask, i).wait_send()
    for j in range(parts):
        for mask in (1, 2, 4):
            x_first(mask, j).wait_send()
        x_relay(j).wait_send()
        for mask in (2, 4, 6):
            x_across(mask, j).wait_send()


def fused(tokens, w_qkv, weight_table, weight_index, cotangent, parts=2, subs=4, lag=3):
    seq = lax.axis_size("seq")
    dp = lax.axis_size("dp")
    block, width = tokens.shape[1:]
    inner_width = w_qkv.shape[2]
    heads = weight_table.shape[1]
    hd = inner_width // heads
    levels = seq.bit_length() - 1
    rows = w_qkv.shape[0]
    groups = weight_index.shape[1]
    bf = jnp.bfloat16
    f32 = jnp.float32
    vm = pltpu.VMEM
    dma = pltpu.SemaphoreType.DMA
    wide = (seq, rows, 3 * hd)
    out, gw = pl.pallas_call(
        functools.partial(fused_kernel, (seq, dp, block, width, hd, groups, levels, parts, subs, lag)),
        out_shape=(
            jax.ShapeDtypeStruct((block, inner_width), bf),
            jax.ShapeDtypeStruct((3, rows, inner_width), bf),
        ),
        in_specs=[
            pl.BlockSpec(memory_space=pl.ANY),
            pl.BlockSpec(memory_space=pl.ANY),
            pl.BlockSpec(memory_space=pltpu.SMEM),
            pl.BlockSpec(memory_space=pltpu.SMEM),
            pl.BlockSpec(memory_space=pl.ANY),
        ],
        out_specs=(pl.BlockSpec(memory_space=pl.ANY),) * 2,
        scratch_shapes=[
            vm((heads, (levels + 1) * groups, hd), f32),
            vm((seq, block, width), bf),
            vm((width, seq * block), bf),
            vm((width, 3 * hd), bf),
            vm((seq, block, hd), bf),
            vm((seq, (levels + 1) * groups, hd), f32),
            vm((seq, block, 3 * hd), bf),
            vm((seq, hd, hd), f32),
            vm((seq, block, 3 * hd), f32),
            vm((seq, block, hd), f32),
            vm((seq, block, hd), bf),
            vm((seq * block, 3 * hd), bf),
            vm((levels, seq, hd, hd), bf),
            vm((levels, seq, hd, hd), f32),
            vm(wide, bf), vm(wide, bf), vm(wide, bf), vm(wide, bf), vm(wide, bf), vm(wide, bf),
            dma((7,)),
            dma((seq, 3)), dma((seq, 3)),
            dma((seq,)), dma((seq,)),
            dma((seq,)), dma((seq,)),
            dma((seq, parts)), dma((seq, parts)),
            dma((seq,)), dma((seq,)),
            dma((seq,)), dma((seq,)),
            dma((seq,)), dma((seq,)),
            dma((seq,)), dma((seq,)),
            dma((seq,)), dma((seq,)),
            dma((seq * subs,)), dma((seq * subs,)),
            dma((seq * subs,)), dma((seq * subs,)),
            dma((seq * subs,)), dma((seq * subs,)),
            dma((seq, 3)),
        ],
        compiler_params=pltpu.CompilerParams(
            collective_id=0, has_side_effects=True, vmem_limit_bytes=60 * 2**20
        ),
        name="fused",
    )(tokens[0], jnp.transpose(w_qkv, (1, 0, 2)), weight_table.T, weight_index[0], cotangent[0])
    return (out[None], jnp.transpose(gw, (1, 0, 2)).astype(f32))


def solution(mesh):
    def body(tokens, w_qkv, weight_table, weight_index, cotangent):
        seq, heads = mesh.shape["seq"], weight_table.shape[1]
        if seq == heads == 8 and mesh.shape["dp"] == 4:
            plan = fused
        elif heads % seq == 0:
            plan = head_parallel
        else:
            plan = per_device
        return plan(tokens, w_qkv, weight_table, weight_index, cotangent)

    return jax.shard_map(
        body,
        mesh=mesh,
        in_specs=(
            P("dp", "seq", None),
            P("seq", None, None),
            P(),
            P("dp", "seq", None),
            P("dp", "seq", None),
        ),
        out_specs=(P("dp", "seq", None), P("seq", None, None)),
        check_vma=False,
    )
```

profile of v0, /device:TPU:0, one launch (start us, length us, event | category | flops | bytes accessed | tf_op | source)
XLA Modules:
  0.0 114.6 jit_solution(2737950982860672291)
XLA Ops:
  0.6 109.7 %fused.1 = (bf16[256,1024]{1,0:T(8,128)(2,1)}, bf16[3,256,1024]{2,1,0:T(8,128)(2,1)}) custom-call(bf16[256,2048]{1,0:T(8,128)(2,1)} %bitcast.9, bf16[3,256,1024]{2,1,0:T(8,128)(2,1)} %bitcast.8, f32[8,16]{1,0:T(8,128)} %bitcast.12, s32[2,4]{1,0:T(2,128)} %bitcast.13, bf16[256,1024]{1,0:T(8,128)(2,1)} %bitcast.11), custom_call_target="tpu_custom_call" | custom-call | tf_op jit(solution)/shard_map/fused/pallas_call | solution.py:691
  110.3 0.0 copy-start
  110.3 3.5 %convert_bitcast_fusion = f32[256,3,1024]{2,0,1:T(8,128)} fusion(bf16[3,256,1024]{2,1,0:T(8,128)(2,1)} %get-tuple-element.5), kind=kLoop, calls=%fused_computation | loop fusion | flops 786432 | bytes 4718592 | tf_op jit(solution)/shard_map/convert_element_type | solution.py:741
  113.8 0.0 copy-done
  113.9 0.8 copy.8
Async XLA Ops:
  110.3 3.5 %copy-start = (bf16[256,1024]{1,0:T(8,128)(2,1)S(1)}, bf16[256,1024]{1,0:T(8,128)(2,1)}, u32[]{:S(2)}) copy-start(bf16[256,1024]{1,0:T(8,128)(2,1)} %get-tuple-element.4) | copy-start | bytes 1572868
where the time goes:
time: 115 us
  Pallas kernels  110 us (96%)
  other arithmetic  3.52 us (3%)
    pallas_call x1, Pallas kernels, fused(): pl.pallas_call(functools.partial(fused_kernel, (seq, dp, block, width, hd...  110 us
    convert_element_type x1, other arithmetic, fused(): return (out[None], jnp.transpose(gw, (1, 0, 2)).astype(f32))  3.52 us

commit v1 on v0

--- a/solution.py
+++ b/solution.py
@@ -231,8 +231,8 @@
     out_ref, gw_ref,
     lam_ref, xs, xt, wh, cs, lam, qkv, st, loc, outf, outb, dqkv, lvl, gl,
     gs, own, leaf, pair, pairb, fin,
-    s_local, s_ws, s_wr, s_cs, s_cr, s_ls, s_lr, s_xs, s_xr, s_os, s_or,
-    s_wa, s_war, s_wb, s_wbr, s_wc, s_wcr, s_gs, s_gr, s_za, s_zar, s_zb, s_zbr, s_zc, s_zcr, s_fin,
+    s_local, s_ws, s_wr, s_c, s_l, s_xs, s_xr, s_o, s_wz, s_war, s_wbr, s_gs, s_gr,
+    s_zs, s_zar, s_zbr, s_fin,
 ):
     seq, dp, block, width, hd, groups, levels, parts, subs, lag = sizes
     bf = jnp.bfloat16
@@ -299,36 +299,41 @@
         return remote(
             w_ref.at[i, pl.ds(pl.multiple_of(start, quarter), count), lanes(peer)],
             wh.at[held(me, start, count), pl.ds(i * hd, hd)],
-            s_ws.at[mask, i], s_wr.at[mask, i], {"seq": peer},
-        )
+            s_ws.at[0], s_wr.at[mask], {"seq": peer},
+        )
+
+    def w_arrived(mask):
+        start, count = (0, rows) if mask == 1 else (z * quarter, quarter)
+        piece = wh.at[held(flip(me, mask), start, count)]
+        return remote(piece, piece, s_ws.at[0], s_wr.at[mask], {"seq": flip(me, mask)})
 
     def wa_copy(mask):
         piece = wh.at[held(flip(me, mask), z * quarter, quarter)]
-        return remote(piece, piece, s_wa.at[mask], s_war.at[mask], {"dp": mate})
+        return remote(piece, piece, s_wz.at[0], s_war.at[mask], {"dp": mate})
 
     def wb_copy(mask):
         piece = wh.at[held(flip(me, mask), side * half_rows, half_rows)]
-        return remote(piece, piece, s_wb.at[mask], s_wbr.at[mask], {"dp": cross})
+        return remote(piece, piece, s_wz.at[0], s_wbr.at[mask], {"dp": cross})
 
     def wc_copy(mask):
         piece = wh.at[held(flip(me, mask), (1 - side) * half_rows, half_rows)]
-        return remote(piece, piece, s_wc.at[mask], s_wcr.at[mask], {"dp": mate})
+        return remote(piece, piece, s_wz.at[0], s_wbr.at[mask], {"dp": mate})
 
     def l_copy(mask):
         peer = flip(me, mask)
-        return remote(lam_ref.at[peer], lam.at[me], s_ls.at[mask], s_lr.at[mask], {"seq": peer})
+        return remote(lam_ref.at[peer], lam.at[me], s_l.at[0], s_l.at[1], {"seq": peer})
 
     def c_copy(mask):
         peer = flip(me, mask)
         return remote(
-            cot_ref.at[:, lanes(peer)], cs.at[me], s_cs.at[mask], s_cr.at[mask], {"seq": peer}
+            cot_ref.at[:, lanes(peer)], cs.at[me], s_c.at[0], s_c.at[1], {"seq": peer}
         )
 
     def x_first(mask, j):
         piece = pl.ds(j * part, part)
         return remote(
             tok_ref.at[piece], xs.at[me, piece],
-            s_xs.at[mask, j], s_xr.at[mask, j], {"seq": flip(me, mask)},
+            s_xs.at[0], s_xr.at[mask, j], {"seq": flip(me, mask)},
         )
 
     def x_relay(j):
@@ -336,7 +341,7 @@
         moved = flip(me, first)
         return remote(
             xs.at[moved, piece], xs.at[moved, piece],
-            s_xs.at[6, j], s_xr.at[6, j], {"seq": flip(me, other)},
+            s_xs.at[0], s_xr.at[6, j], {"seq": flip(me, other)},
         )
 
     def x_across(mask, j):
@@ -344,7 +349,7 @@
         moved = flip(me, mask)
         return remote(
             xs.at[moved, piece], xs.at[moved, piece],
-            s_xs.at[mask + 1, j], s_xr.at[mask + 1, j], {"seq": flip(me, 1)},
+            s_xs.at[0], s_xr.at[mask + 1, j], {"seq": flip(me, 1)},
         )
 
     def x_arrived(mask, j):
@@ -352,21 +357,23 @@
         moved = flip(me, mask)
         return remote(
             xs.at[moved, piece], xs.at[moved, piece],
-            s_xs.at[0, j], s_xr.at[mask, j], {"seq": flip(me, 1)},
-        )
+            s_xs.at[0], s_xr.at[mask, j], {"seq": flip(me, 1)},
+        )
+
+    def together(piece, sends, receives):
+        return remote(piece, piece, sends, receives, {"seq": flip(me, 1)})
 
     locals_ = [
         pltpu.make_async_copy(tok_ref, xs.at[me], s_local.at[0]),
         pltpu.make_async_copy(cot_ref.at[:, lanes(me)], cs.at[me], s_local.at[1]),
         pltpu.make_async_copy(lam_ref.at[me], lam.at[me], s_local.at[2]),
     ]
-    for i in range(3):
-        locals_.append(
-            pltpu.make_async_copy(
-                w_ref.at[i, :, lanes(me)], wh.at[span(me, rows), pl.ds(i * hd, hd)],
-                s_local.at[3 + i],
-            )
-        )
+    w_locals = [
+        pltpu.make_async_copy(
+            w_ref.at[i, :, lanes(me)], wh.at[span(me, rows), pl.ds(i * hd, hd)], s_local.at[3]
+        )
+        for i in range(3)
+    ]
     order = (6, 7, 2, 3, 4, 5, 1)
     for mask in order:
         l_copy(mask).start()
@@ -377,15 +384,21 @@
     for j in range(parts):
         for mask in (2, 4, 1):
             x_first(mask, j).start()
-    for copy in locals_:
+    for copy in locals_ + w_locals:
         copy.start()
     for copy in locals_:
         copy.wait()
+    own_w = wh.at[span(me, rows)]
+    pltpu.make_async_copy(own_w, own_w, s_local.at[3]).wait()
     far_masks = order[:-1]
     for mask in far_masks:
-        for i in range(3):
-            w_copy(mask, i).wait_recv()
+        w_arrived(mask).wait_recv()
         wa_copy(mask).start()
+
+    def relay(j):
+        x_arrived(first, j).wait_recv()
+        x_relay(j).start()
+        x_across(first, j).start()
 
     @pl.when(inner)
     def _():
@@ -396,6 +409,8 @@
             wb_copy(mask).wait_recv()
             wc_copy(mask).start()
 
+    relay(0)
+
     @pl.when(jnp.logical_not(inner))
     def _():
         for mask in far_masks:
@@ -403,11 +418,9 @@
         for mask in far_masks:
             wc_copy(mask).wait_recv()
 
-    for i in range(3):
-        w_copy(1, i).wait_recv()
-    for mask in order:
-        l_copy(mask).wait_recv()
-        c_copy(mask).wait_recv()
+    w_arrived(1).wait_recv()
+    together(lam.at[pl.ds(0, seq - 1)], s_l.at[0], s_l.at[1]).wait_recv()
+    together(cs.at[pl.ds(0, seq - 1)], s_c.at[0], s_c.at[1]).wait_recv()
 
     tri = lax.broadcasted_iota(jnp.int32, (block, block), 0) >= lax.broadcasted_iota(
         jnp.int32, (block, block), 1
@@ -440,9 +453,8 @@
         @pl.when(i == 2)
         def _():
             for j in range(parts):
-                x_arrived(first, j).wait_recv()
-                x_relay(j).start()
-                x_across(first, j).start()
+                if j > 0:
+                    relay(j)
                 x_arrived(other, j).wait_recv()
                 x_across(other, j).start()
 
@@ -493,7 +505,7 @@
     def o_copy(mask):
         peer = flip(me, mask)
         return remote(
-            outb.at[peer], out_ref.at[:, lanes(me)], s_os.at[mask], s_or.at[mask], {"seq": peer}
+            outb.at[peer], out_ref.at[:, lanes(me)], s_o.at[0], s_o.at[1], {"seq": peer}
         )
 
     blank = jnp.zeros((hd, hd), bf)
@@ -521,10 +533,7 @@
             gl[level - 1, base] = total
     for p in range(seq):
         outb[p] = outf[p].astype(bf)
-    for mask in range(1, seq):
-        o_copy(mask).start()
-    o_local = pltpu.make_async_copy(outb.at[me], out_ref.at[:, lanes(me)], s_local.at[6])
-    o_local.start()
+    o_local = pltpu.make_async_copy(outb.at[me], out_ref.at[:, lanes(me)], s_local.at[0])
     for p in range(seq):
         total = None
         for level in range(1, levels + 1):
@@ -542,33 +551,36 @@
         dqkv[spot, pl.ds(0, hd)] = loc[p, :, pl.ds(0, hd)].astype(bf)
         dqkv[spot, pl.ds(hd, 2 * hd)] = grads.astype(bf)
 
+    def pick(k):
+        return k + jnp.where(k == 3, 1, 0) - jnp.where(k == 4, 1, 0)
+
     def g_copy(m):
-        return remote(gs.at[m], own.at[m], s_gs.at[m], s_gr.at[m], {"seq": flip(me, m)})
+        return remote(gs.at[m], own.at[m], s_gs.at[0], s_gr.at[m], {"seq": flip(me, m)})
 
     def bit_of(r):
         return pl.ds(pl.multiple_of(lax.rem(r, subs) * piece_rows, piece_rows), piece_rows)
 
     def za_copy(r):
-        m, at = lax.div(r, subs), bit_of(r)
-        return remote(own.at[m, at], leaf.at[m, at], s_za.at[r], s_zar.at[r], {"dp": mate})
+        m, at = pick(lax.div(r, subs)), bit_of(r)
+        return remote(own.at[m, at], leaf.at[m, at], s_zs.at[0], s_zar.at[r], {"dp": mate})
 
     def zb_copy(r):
-        m, at = lax.div(r, subs), bit_of(r)
-        return remote(pair.at[m, at], pairb.at[m, at], s_zb.at[r], s_zbr.at[r], {"dp": cross})
+        m, at = pick(lax.div(r, subs)), bit_of(r)
+        return remote(pair.at[m, at], pairb.at[m, at], s_zs.at[0], s_zbr.at[r], {"dp": cross})
 
     def zc_copy(r):
-        m, at = lax.div(r, subs), bit_of(r)
-        return remote(fin.at[m, at], fin.at[m, at], s_zc.at[r], s_zcr.at[r], {"dp": mate})
+        m, at = pick(lax.div(r, subs)), bit_of(r)
+        return remote(fin.at[m, at], fin.at[m, at], s_zs.at[1], s_zar.at[r], {"dp": mate})
 
     def fin_copy(m, i):
         return pltpu.make_async_copy(
-            fin.at[m, :, pl.ds(i * hd, hd)], gw_ref.at[i, :, lanes(flip(me, m))], s_fin.at[m, i]
+            fin.at[m, :, pl.ds(i * hd, hd)], gw_ref.at[i, :, lanes(flip(me, m))], s_fin.at[0]
         )
 
     steps = seq * subs
 
     def reduce_round(t, carry):
-        m = lax.div(t, subs)
+        m = pick(lax.div(t, subs))
 
         @pl.when((t < steps) & (lax.rem(t, subs) == 0))
         def _():
@@ -584,10 +596,16 @@
                 gs[m] = chunk
                 g_copy(m).start()
 
+            @pl.when(m == seq - 1)
+            def _():
+                for mask in range(1, seq):
+                    o_copy(mask).start()
+                o_local.start()
+
         @pl.when((t >= subs) & (t < steps + subs))
         def _():
             r = t - subs
-            done = lax.div(r, subs)
+            done = pick(lax.div(r, subs))
             at = bit_of(r)
 
             @pl.when((r >= subs) & (lax.rem(r, subs) == 0))
@@ -607,7 +625,7 @@
         @pl.when((t >= subs + lag) & inner)
         def _():
             r = t - subs - lag
-            done = lax.div(r, subs)
+            done = pick(lax.div(r, subs))
             at = bit_of(r)
             zb_copy(r).wait_recv()
             fin[done, at] = (pair[done, at].astype(f32) + pairb[done, at].astype(f32)).astype(bf)
@@ -622,55 +640,39 @@
 
     lax.fori_loop(0, steps + subs + lag, reduce_round, 0)
 
+    everything = fin.at[...]
+
     @pl.when(jnp.logical_not(inner))
     def _():
-        def collect(m, carry):
+        def collect(k, carry):
+            m = pick(k)
             for b in range(subs):
-                zc_copy(m * subs + b).wait_recv()
+                zc_copy(k * subs + b).wait_recv()
             for i in range(3):
                 fin_copy(m, i).start()
-            for b in range(subs):
-                za_copy(m * subs + b).wait_send()
             return carry
 
         lax.fori_loop(0, seq, collect, 0)
+        together(everything, s_zs.at[0], s_zar.at[0]).wait_send()
+        together(wh.at[pl.ds(0, 6 * quarter)], s_wz.at[0], s_war.at[0]).wait_send()
 
     @pl.when(inner)
     def _():
-        def settle(r, carry):
-            zb_copy(r).wait_send()
-            zc_copy(r).wait_send()
-            return carry
-
-        lax.fori_loop(0, steps, settle, 0)
-
-    for mask in far_masks:
-        wa_copy(mask).wait_send()
-
-    @pl.when(inner)
-    def _():
-        for mask in far_masks:
-            wb_copy(mask).wait_send()
-            wc_copy(mask).wait_send()
-
-    for m in range(seq):
-        for i in range(3):
-            fin_copy(m, i).wait()
+        together(everything, s_zs.at[0], s_zar.at[0]).wait_send()
+        together(everything, s_zs.at[1], s_zar.at[0]).wait_send()
+        moved = 6 * (quarter + 2 * half_rows)
+        together(wh.at[pl.ds(0, moved)], s_wz.at[0], s_war.at[0]).wait_send()
+
+    pltpu.make_async_copy(everything, everything, s_fin.at[0]).wait()
     o_local.wait()
-    for mask in range(1, seq):
-        o_copy(mask).wait_send()
-        o_copy(mask).wait_recv()
-        g_copy(mask).wait_send()
-        l_copy(mask).wait_send()
-        c_copy(mask).wait_send()
-        for i in range(3):
-            w_copy(mask, i).wait_send()
-    for j in range(parts):
-        for mask in (1, 2, 4):
-            x_first(mask, j).wait_send()
-        x_relay(j).wait_send()
-        for mask in (2, 4, 6):
-            x_across(mask, j).wait_send()
+    most = pl.ds(0, seq - 1)
+    together(outb.at[most], s_o.at[0], s_o.at[1]).wait_send()
+    together(outb.at[most], s_o.at[0], s_o.at[1]).wait_recv()
+    together(gs.at[most], s_gs.at[0], s_gr.at[0]).wait_send()
+    together(lam_ref.at[most], s_l.at[0], s_l.at[1]).wait_send()
+    together(cs.at[most], s_c.at[0], s_c.at[1]).wait_send()
+    together(wh.at[pl.ds(0, 6 * quarter + rows)], s_ws.at[0], s_wr.at[0]).wait_send()
+    together(xs.at[most], s_xs.at[0], s_xr.at[0, 0]).wait_send()
 
 
 def fused(tokens, w_qkv, weight_table, weight_index, cotangent, parts=2, subs=4, lag=3):
@@ -718,20 +720,16 @@
             vm((levels, seq, hd, hd), bf),
             vm((levels, seq, hd, hd), f32),
             vm(wide, bf), vm(wide, bf), vm(wide, bf), vm(wide, bf), vm(wide, bf), vm(wide, bf),
-            dma((7,)),
-            dma((seq, 3)), dma((seq, 3)),
-            dma((seq,)), dma((seq,)),
-            dma((seq,)), dma((seq,)),
-            dma((seq, parts)), dma((seq, parts)),
-            dma((seq,)), dma((seq,)),
-            dma((seq,)), dma((seq,)),
-            dma((seq,)), dma((seq,)),
-            dma((seq,)), dma((seq,)),
-            dma((seq,)), dma((seq,)),
-            dma((seq * subs,)), dma((seq * subs,)),
-            dma((seq * subs,)), dma((seq * subs,)),
-            dma((seq * subs,)), dma((seq * subs,)),
-            dma((seq, 3)),
+            dma((4,)),
+            dma((1,)), dma((seq,)),
+            dma((2,)),
+            dma((2,)),
+            dma((1,)), dma((seq, parts)),
+            dma((2,)),
+            dma((1,)), dma((seq,)), dma((seq,)),
+            dma((1,)), dma((seq,)),
+            dma((2,)), dma((seq * subs,)), dma((seq * subs,)),
+            dma((1,)),
         ],
         compiler_params=pltpu.CompilerParams(
             collective_id=0, has_side_effects=True, vmem_limit_bytes=60 * 2**20

time: 115 us -> 110 us (0.957)
  Pallas kernels: 110 us -> 104 us
    pallas_call x1, Pallas kernels: 110 us -> 104 us  [fused(): pl.pallas_call(functools.partial(fused_kernel, (seq, dp, block, width, hd...]
where the time goes in v1:
time: 110 us; the launch traced here: 109 us
  Pallas kernels  104 us (95%)
  other arithmetic  3.52 us (3%)
    pallas_call x1, Pallas kernels, fused(): pl.pallas_call(functools.partial(fused_kernel, (seq, dp, block, width, hd...  104 us
    convert_element_type x1, other arithmetic, fused(): return (out[None], jnp.transpose(gw, (1, 0, 2)).astype(f32))  3.52 us

profile of v1, /device:TPU:0, one launch (start us, length us, event | category | flops | bytes accessed | tf_op | source)
XLA Modules:
  0.0 109.0 jit_solution(2880195906030587197)
XLA Ops:
  0.6 104.0 %fused.1 = (bf16[256,1024]{1,0:T(8,128)(2,1)}, bf16[3,256,1024]{2,1,0:T(8,128)(2,1)}) custom-call(bf16[256,2048]{1,0:T(8,128)(2,1)} %bitcast.9, bf16[3,256,1024]{2,1,0:T(8,128)(2,1)} %bitcast.8, f32[8,16]{1,0:T(8,128)} %bitcast.12, s32[2,4]{1,0:T(2,128)} %bitcast.13, bf16[256,1024]{1,0:T(8,128)(2,1)} %bitcast.11), custom_call_target="tpu_custom_call" | custom-call | tf_op jit(solution)/shard_map/fused/pallas_call | solution.py:693
  104.6 0.0 copy-start
  104.7 3.5 %convert_bitcast_fusion = f32[256,3,1024]{2,0,1:T(8,128)} fusion(bf16[3,256,1024]{2,1,0:T(8,128)(2,1)} %get-tuple-element.5), kind=kLoop, calls=%fused_computation | loop fusion | flops 786432 | bytes 4718592 | tf_op jit(solution)/shard_map/convert_element_type | solution.py:739
  108.2 0.0 copy-done
  108.2 0.8 copy.8
Async XLA Ops:
  104.6 3.5 %copy-start = (bf16[256,1024]{1,0:T(8,128)(2,1)S(1)}, bf16[256,1024]{1,0:T(8,128)(2,1)}, u32[]{:S(2)}) copy-start(bf16[256,1024]{1,0:T(8,128)(2,1)} %get-tuple-element.4) | copy-start | bytes 1572868

commit v2 on v1

--- a/solution.py
+++ b/solution.py
@@ -234,7 +234,7 @@
     s_local, s_ws, s_wr, s_c, s_l, s_xs, s_xr, s_o, s_wz, s_war, s_wbr, s_gs, s_gr,
     s_zs, s_zar, s_zbr, s_fin,
 ):
-    seq, dp, block, width, hd, groups, levels, parts, subs, lag = sizes
+    seq, dp, block, width, hd, groups, levels, parts, subs, lag, ahead = sizes
     bf = jnp.bfloat16
     f32 = jnp.float32
     me = lax.axis_index("seq")
@@ -579,66 +579,79 @@
 
     steps = seq * subs
 
-    def reduce_round(t, carry):
-        m = pick(lax.div(t, subs))
-
-        @pl.when((t < steps) & (lax.rem(t, subs) == 0))
-        def _():
-            o = flip(me, m)
-            chunk = dims(xt[span(o, rows), :], dqkv[...], 1, 0).astype(bf)
-
-            @pl.when(m == 0)
+    def make_chunk(m):
+        o = flip(me, m)
+        chunk = dims(xt[span(o, rows), :], dqkv[...], 1, 0).astype(bf)
+
+        @pl.when(m == 0)
+        def _():
+            own[0] = chunk
+
+        @pl.when(m > 0)
+        def _():
+            gs[m] = chunk
+            g_copy(m).start()
+
+        @pl.when(m == seq - 1)
+        def _():
+            for mask in range(1, seq):
+                o_copy(mask).start()
+            o_local.start()
+
+    def prepare(k, carry):
+        make_chunk(pick(k))
+
+        @pl.when((k == 0) & jnp.logical_not(inner))
+        def _():
+            for r in range(subs):
+                za_copy(r).start()
+
+        return carry
+
+    lax.fori_loop(0, ahead, prepare, 0)
+
+    def reduce_round(r, carry):
+        k = lax.div(r, subs)
+
+        @pl.when((k < seq - ahead) & (lax.rem(r, subs) == 0))
+        def _():
+            make_chunk(pick(k + ahead))
+
+        @pl.when((r >= subs) & (r < steps))
+        def _():
+            @pl.when(lax.rem(r, subs) == 0)
             def _():
-                own[0] = chunk
-
-            @pl.when(m > 0)
-            def _():
-                gs[m] = chunk
-                g_copy(m).start()
-
-            @pl.when(m == seq - 1)
-            def _():
-                for mask in range(1, seq):
-                    o_copy(mask).start()
-                o_local.start()
-
-        @pl.when((t >= subs) & (t < steps + subs))
-        def _():
-            r = t - subs
-            done = pick(lax.div(r, subs))
-            at = bit_of(r)
-
-            @pl.when((r >= subs) & (lax.rem(r, subs) == 0))
-            def _():
-                g_copy(done).wait_recv()
+                g_copy(pick(k)).wait_recv()
 
             @pl.when(jnp.logical_not(inner))
             def _():
                 za_copy(r).start()
 
-            @pl.when(inner)
-            def _():
-                za_copy(r).wait_recv()
-                pair[done, at] = (own[done, at].astype(f32) + leaf[done, at].astype(f32)).astype(bf)
-                zb_copy(r).start()
-
-        @pl.when((t >= subs + lag) & inner)
-        def _():
-            r = t - subs - lag
-            done = pick(lax.div(r, subs))
+        @pl.when((r < steps) & inner)
+        def _():
+            done = pick(k)
             at = bit_of(r)
-            zb_copy(r).wait_recv()
+            za_copy(r).wait_recv()
+            pair[done, at] = (own[done, at].astype(f32) + leaf[done, at].astype(f32)).astype(bf)
+            zb_copy(r).start()
+
+        @pl.when((r >= lag) & inner)
+        def _():
+            back = r - lag
+            done = pick(lax.div(back, subs))
+            at = bit_of(back)
+            zb_copy(back).wait_recv()
             fin[done, at] = (pair[done, at].astype(f32) + pairb[done, at].astype(f32)).astype(bf)
-            zc_copy(r).start()
-
-            @pl.when(lax.rem(r, subs) == subs - 1)
+            zc_copy(back).start()
+
+            @pl.when(lax.rem(back, subs) == subs - 1)
             def _():
                 for i in range(3):
                     fin_copy(done, i).start()
 
         return carry
 
-    lax.fori_loop(0, steps + subs + lag, reduce_round, 0)
+    lax.fori_loop(0, steps + lag, reduce_round, 0)
 
     everything = fin.at[...]
 
@@ -675,7 +688,7 @@
     together(xs.at[most], s_xs.at[0], s_xr.at[0, 0]).wait_send()
 
 
-def fused(tokens, w_qkv, weight_table, weight_index, cotangent, parts=2, subs=4, lag=3):
+def fused(tokens, w_qkv, weight_table, weight_index, cotangent, parts=2, subs=4, lag=3, ahead=3):
     seq = lax.axis_size("seq")
     dp = lax.axis_size("dp")
     block, width = tokens.shape[1:]
@@ -691,7 +704,7 @@
     dma = pltpu.SemaphoreType.DMA
     wide = (seq, rows, 3 * hd)
     out, gw = pl.pallas_call(
-        functools.partial(fused_kernel, (seq, dp, block, width, hd, groups, levels, parts, subs, lag)),
+        functools.partial(fused_kernel, (seq, dp, block, width, hd, groups, levels, parts, subs, lag, ahead)),
         out_shape=(
             jax.ShapeDtypeStruct((block, inner_width), bf),
             jax.ShapeDtypeStruct((3, rows, inner_width), bf),

time: 110 us -> 107 us (0.973)
  Pallas kernels: 104 us -> 102 us
    pallas_call x1, Pallas kernels: 104 us -> 102 us  [fused(): pl.pallas_call(functools.partial(fused_kernel, (seq, dp, block, width, hd...]
where the time goes in v2:
time: 107 us
  Pallas kernels  102 us (95%)
  other arithmetic  3.52 us (3%)
    pallas_call x1, Pallas kernels, fused(): pl.pallas_call(functools.partial(fused_kernel, (seq, dp, block, width, hd...  102 us
    convert_element_type x1, other arithmetic, fused(): return (out[None], jnp.transpose(gw, (1, 0, 2)).astype(f32))  3.52 us

profile of v2, /device:TPU:0, one launch (start us, length us, event | category | flops | bytes accessed | tf_op | source)
XLA Modules:
  0.0 107.0 jit_solution(1867214168063372359)
XLA Ops:
  0.6 102.0 %fused.1 = (bf16[256,1024]{1,0:T(8,128)(2,1)}, bf16[3,256,1024]{2,1,0:T(8,128)(2,1)}) custom-call(bf16[256,2048]{1,0:T(8,128)(2,1)} %bitcast.9, bf16[3,256,1024]{2,1,0:T(8,128)(2,1)} %bitcast.8, f32[8,16]{1,0:T(8,128)} %bitcast.12, s32[2,4]{1,0:T(2,128)} %bitcast.13, bf16[256,1024]{1,0:T(8,128)(2,1)} %bitcast.11), custom_call_target="tpu_custom_call" | custom-call | tf_op jit(solution)/shard_map/fused/pallas_call | solution.py:706
  102.6 0.0 copy-start
  102.7 3.5 %convert_bitcast_fusion = f32[256,3,1024]{2,0,1:T(8,128)} fusion(bf16[3,256,1024]{2,1,0:T(8,128)(2,1)} %get-tuple-element.5), kind=kLoop, calls=%fused_computation | loop fusion | flops 786432 | bytes 4718592 | tf_op jit(solution)/shard_map/convert_element_type | solution.py:752
  106.2 0.0 copy-done
  106.2 0.8 copy.8
Async XLA Ops:
  102.6 3.5 %copy-start = (bf16[256,1024]{1,0:T(8,128)(2,1)S(1)}, bf16[256,1024]{1,0:T(8,128)(2,1)}, u32[]{:S(2)}) copy-start(bf16[256,1024]{1,0:T(8,128)(2,1)} %get-tuple-element.4) | copy-start | bytes 1572868
